TPU v7x, 32 devices: a whole 2x2x4 slice. The times are simulated.
32 devices in a mesh: rep: 2 (over y), seq: 4 (over z), head: 4 (over x, core).
Axes of the slice: x: 2, y: 2, z: 4, core: 2. Of those that a mesh axis runs over, the one named last changes fastest.
Arguments:
- queries: bfloat16 [2, 8, 64, 128], P(None, 'rep', 'head'), parts along dimension 1, may hold values from -22 to 22
- cache_keys: bfloat16 [8, 8, 4096, 128], P('rep', 'head', 'seq'), parts along dimension 0, may hold values from -15 to 15
- cache_values: bfloat16 [8, 8, 4096, 128], P('rep', 'head', 'seq'), parts along dimension 0, may hold values from -24 to 24
- new_keys: bfloat16 [2, 8, 8, 128], P(None, 'rep', 'head'), parts along dimension 1, may hold values from -12 to 12
- new_values: bfloat16 [2, 8, 8, 128], P(None, 'rep', 'head'), parts along dimension 1, may hold values from -24 to 24
- w_out: bfloat16 [8192, 8192], P('head', 'seq'), may hold values from -0.09375 to 0.09375
- lengths: int32 [8], P('rep'), parts along dimension 0, may hold values from 1024 to 4096, as said below
- positions: int32 [8], P('rep'), parts along dimension 0, may hold values from 1024 to 8192, as said below
Outputs:
- layer_out: bfloat16 [2, 8, 8192], P(None, 'rep', ('seq', 'head')), parts along dimension 1
- cache_mass: float32 [8, 8, 4096], P('rep', 'head', 'seq'), parts along dimension 0
- new_mass: float32 [8, 8, 2], P('rep', 'head'), parts along dimension 0
There are 2 independent parts, one for each index of `rep`. A program takes and returns all parts, laid end to end along the dimension named above; an argument that names none is the same for every part. Nothing has to cross between parts.
Inputs may be any that keep to these rules, and one draw needn't show every extreme that they name: `lengths`: at least 1024; in every draw some request holds all 4096 slots. `positions`: each at least its request's cached length; the second new token stands one position further; in every draw some request's first new token stands at 8192.
All inputs are finite; a program needn't handle non-finite values.
Results may differ from a plain program's by a relative error of at most 0.013.
Values sent between devices are 32-bit elements; how exact they have to be, the bound alone decides.
A program may use at most 64 MiB of HBM per device.

v0:
```python
import math

import jax
import jax.numpy as jnp
from jax import lax
from jax.sharding import PartitionSpec as P

ROPE_BASE = 500000.0
FLOOR_SCORE = -1e30


def rotate(values, turns):
    half_dim = values.shape[-1] // 2
    inv_freq = ROPE_BASE ** (-(jnp.arange(half_dim, dtype=jnp.float32) * 2.0 / values.shape[-1]))
    angles = turns[..., None] * inv_freq
    cosine = jnp.cos(angles)
    sine_part = jnp.sin(angles)
    front_half = values[..., :half_dim]
    back_half = values[..., half_dim:]
    return jnp.concatenate(
        [front_half * cosine - back_half * sine_part, back_half * cosine + front_half * sine_part],
        axis=-1,
    )


def body(queries, cache_keys, cache_values, new_keys, new_values, w_out, lengths, positions):
    steps_n, requests, heads_here, head_dim = queries.shape
    kv_here = cache_keys.shape[1]
    group_size = heads_here // kv_here
    local_len = cache_keys.shape[2]
    offsets = jnp.arange(steps_n, dtype=jnp.int32)
    moments = (positions[None, :] + offsets[:, None]).astype(jnp.float32)
    q_turned = rotate(queries.astype(jnp.float32), moments[:, :, None]).astype(jnp.bfloat16)
    k_turned = rotate(new_keys.astype(jnp.float32), moments[:, :, None]).astype(jnp.bfloat16)
    grouped = q_turned.reshape(steps_n, requests, kv_here, group_size, head_dim)
    inv_root = 1.0 / math.sqrt(head_dim)
    key_slots = lax.axis_index("seq") * local_len + jnp.arange(local_len, dtype=jnp.int32)
    in_cache = key_slots[None, :] < lengths[:, None]
    cache_mask = in_cache[None, :, None, None, :]
    visible = offsets[None, :] <= offsets[:, None]
    scores = (
        jnp.einsum("srkgd,rktd->srkgt", grouped, cache_keys, preferred_element_type=jnp.float32)
        * inv_root
    )
    scores = jnp.where(cache_mask, scores, FLOOR_SCORE)
    recent_mask = visible[:, None, None, None, :]
    recent = (
        jnp.einsum("srkgd,jrkd->srkgj", grouped, k_turned, preferred_element_type=jnp.float32)
        * inv_root
    )
    recent = jnp.where(recent_mask, recent, FLOOR_SCORE)
    local_top = jnp.max(scores, axis=-1)
    cache_top = lax.pmax(local_top, "seq")
    highest = jnp.maximum(cache_top, jnp.max(recent, axis=-1))
    weights = jnp.where(cache_mask, jnp.exp(scores - highest[..., None]), 0.0)
    local_values = jnp.einsum(
        "srkgt,rktd->srkgd",
        weights.astype(jnp.bfloat16),
        cache_values,
        preferred_element_type=jnp.float32,
    )
    cache_total, value_total = lax.psum((jnp.sum(weights, axis=-1), local_values), "seq")
    recent_weights = jnp.where(recent_mask, jnp.exp(recent - highest[..., None]), 0.0)
    totals = cache_total + jnp.sum(recent_weights, axis=-1)
    recent_values = jnp.einsum(
        "srkgj,jrkd->srkgd",
        recent_weights.astype(jnp.bfloat16),
        new_values,
        preferred_element_type=jnp.float32,
    )
    attended = ((value_total + recent_values) / totals[..., None]).astype(jnp.bfloat16)
    cache_share = jnp.sum(weights / totals[..., None], axis=(0, 3))
    recent_share = jnp.sum(recent_weights / totals[..., None], axis=(0, 3))
    attended, cache_share, recent_share = (attended, cache_share, recent_share)
    share = lengths.astype(jnp.float32) / (steps_n * group_size)
    cache_mass = cache_share * share[:, None, None]
    new_mass = recent_share * share[:, None, None]
    flattened = attended.reshape(steps_n * requests, heads_here * head_dim)
    summed = lax.psum_scatter(
        lax.dot_general(
            w_out, flattened, (((0,), (1,)), ((), ())), preferred_element_type=jnp.float32
        ),
        "head",
        scatter_dimension=0,
        tiled=True,
    )
    layer_out = summed.T.reshape(steps_n, requests, -1).astype(jnp.bfloat16)
    return (layer_out, cache_mass, new_mass)


def solution(mesh):
    return jax.shard_map(
        body,
        mesh=mesh,
        in_specs=(
            P(None, "rep", "head", None),
            P("rep", "head", "seq", None),
            P("rep", "head", "seq", None),
            P(None, "rep", "head", None),
            P(None, "rep", "head", None),
            P("head", "seq"),
            P("rep"),
            P("rep"),
        ),
        out_specs=(
            P(None, "rep", ("seq", "head")),
            P("rep", "head", "seq"),
            P("rep", "head", None),
        ),
        check_vma=False,
    )
```

profile of v0, /device:TPU:0, one launch (start us, length us, event | category | flops | bytes accessed | tf_op | source)
XLA Modules:
  0.0 95.0 jit_solution(5185574436190874566)
XLA Ops:
  7.2 0.0 copy-start
  7.2 0.0 all-reduce.2.cloned.1.call-start
  7.3 0.9 add_convert_fusion.2
  8.1 0.1 multiply_cosine_fusion
  8.3 0.8 convert_element_type.37
  9.1 0.7 copy_convert_fusion
  9.7 0.1 subtract_convert_fusion.1
  9.8 0.7 broadcast_compare_fusion
  10.6 0.1 fusion.27
  10.7 0.0 copy-done
  10.7 0.8 fusion.38
  11.5 0.0 copy-start.1
  11.5 13.9 %pmax.7 = f32[2,4,2,8]{3,0,2,1:T(2,128)S(1)} all-reduce(f32[2,4,2,8]{3,0,2,1:T(2,128)S(1)} %get-tuple-element.12), channel_id=1, replica_groups=mesh['rep'=2,'seq'=4,'head'=4] {'seq'}, use_global_device_ids=true, to_apply=%region_1.2 | all-reduce | flops 128 | bytes 1024 | tf_op jit(solution)/shard_map/pmax | solution.py:53
  25.3 0.0 copy-start.2
  25.3 0.4 fusion.39
  25.7 2.7 %fusion.15 = f32[2,4,2,8,128]{4,3,0,2,1:T(8,128)} fusion(bf16[4,2,1024,128]{3,2,1,0:T(8,128)(2,1)} %param.10, f32[2,4,2,8,1024]{4,3,0,2,1:T(8,128)S(1)} %get-tuple-element.13, f32[2,4,2,8]{3,0,2,1:T(2,128)S(1)} %max.5, pred[4,1024]{1,0:T(4,128)(4,1)S(1)} %broadcast_compare_fusion), kind=kOutput, calls=%fused_computation.11 | convolution fusion | flops 33947648 | bytes 2691584 | tf_op jit(solution)/shard_map/srkgt,rktd->srkgd/dot_general | solution.py:56
  28.4 0.0 all-reduce.2.cloned.1.call-update
  28.4 0.0 reduce-scatter.2.cloned.1.call-start
  28.5 0.3 fusion.21
  28.7 0.0 copy-done.1
  28.7 0.1 fusion.37
  28.8 8.5 %psum.15 = f32[2,4,2,8]{3,0,2,1:T(2,128)S(1)} all-reduce(f32[2,4,2,8]{3,0,2,1:T(2,128)S(1)} %fusion.21), channel_id=1, replica_groups=mesh['rep'=2,'seq'=4,'head'=4] {'seq'}, use_global_device_ids=true, to_apply=%region_5.6 | all-reduce | flops 128 | bytes 1024 | tf_op jit(solution)/shard_map/psum | solution.py:62
  37.4 0.2 divide_reduce_fusion.1
  37.5 0.1 broadcast_multiply_fusion.1
  37.6 0.3 divide_reduce_fusion
  37.9 0.7 copy.29
  38.6 22.5 %all-reduce.2.cloned.1.call-done = f32[2,4,2,8,128]{4,3,0,2,1:T(8,128)} async-done(((f32[2,4,2,8,128]{4,3,0,2,1:T(8,128)}), f32[2,4,2,8,128]{4,3,0,2,1:T(8,128)}) %all-reduce.2.cloned.1.call-update) | async-done | bytes 65552 | tf_op jit(solution)/shard_map/psum | solution.py:62
  61.1 0.0 copy-done.2
  61.1 1.1 %fusion.18 = bf16[2,4,2,8,128]{4,3,0,2,1:T(8,128)(2,1)S(1)} fusion(f32[2,4,2,8,128]{4,3,0,2,1:T(8,128)} %all-reduce.2.cloned.1.call-done, f32[2,4,2,8]{3,0,2,1:T(2,128)S(1)} %add.53, bf16[2,4,2,128,1]{3,2,1,0,4:T(2,128)(2,1)S(1)} %bitcast.56, f32[2,4,2,8,2]{3,4,0,2,1:T(2,128)S(1)} %get-tuple-element.15, pred[2,2]{1,0:T(4,128)(4,1)S(1)} %iota_compare_fusion, ...), kind=kOutput, calls=%fused_computation.12 | convolution fusion | flops 115456 | bytes 104452 | tf_op jit(solution)/shard_map/srkgj,jrkd->srkgd/dot_general | solution.py:65
  62.2 5.2 %convolution_bitcast_fusion = f32[2048,8]{0,1:T(8,128)} fusion(bf16[8,2048]{1,0:T(8,128)(2,1)S(1)} %reshape.95, bf16[2048,2048]{1,0:T(8,128)(2,1)} %param.13), kind=kOutput, calls=%fused_computation | convolution fusion | flops 67108864 | bytes 8486912 | tf_op jit(solution)/shard_map/dot_general | solution.py:80
  67.4 0.0 reduce-scatter.2.cloned.1.call-update
  67.5 0.7 broadcast_multiply_fusion
  68.2 18.7 %reduce-scatter.2.cloned.1.call-done = f32[512,8]{0,1:T(8,128)} async-done(((f32[2048,8]{0,1:T(8,128)}), f32[512,8]{0,1:T(8,128)}) %reduce-scatter.2.cloned.1.call-update) | async-done | bytes 16400 | tf_op jit(solution)/shard_map/reduce_scatter | solution.py:79
  86.9 0.7 convert_bitcast_fusion
  87.6 0.6 convert_element_type.45
  (10 shorter events, 0.1 us)
Async XLA Ops:
  7.2 3.5 %copy-start = (bf16[4,2,1024,128]{3,2,1,0:T(8,128)(2,1)S(1)}, bf16[4,2,1024,128]{3,2,1,0:T(8,128)(2,1)}, u32[]{:S(2)}) copy-start(bf16[4,2,1024,128]{3,2,1,0:T(8,128)(2,1)} %param.9) | copy-start | bytes 6291460
  7.2 53.9 %all-reduce.2.cloned.1.call-start = ((), (), s32[]{:S(2)}) async-start(), calls=%async_computation.1 | async-start | bytes 131072 | tf_op jit(solution)/shard_map/psum | solution.py:62
  11.5 17.3 %copy-start.1 = (s32[4]{0:T(128)S(1)}, s32[4]{0:T(128)}, u32[]{:S(2)}) copy-start(s32[4]{0:T(128)} %param.14) | copy-start | bytes 52
  25.3 35.8 %copy-start.2 = (bf16[2,4,2,128]{3,2,1,0:T(2,128)(2,1)S(1)}, bf16[2,4,2,128]{3,2,1,0:T(2,128)(2,1)}, u32[]{:S(2)}) copy-start(bf16[2,4,2,128]{3,2,1,0:T(2,128)(2,1)} %param.12) | copy-start | bytes 12292
  28.4 58.4 %reduce-scatter.2.cloned.1.call-start = ((), (), s32[]{:S(2)}) async-start(), calls=%async_computation.2 | async-start | bytes 81920 | tf_op jit(solution)/shard_map/reduce_scatter | solution.py:79
Sparse Core Ops, SparseCore 0:
  28.5 32.5 all-reduce.1
  67.6 19.2 reduce-scatter.1
where the time goes:
time: 95.4 us; the launch traced here: 95 us
  waiting for transfers between devices  41.2 us (43%)
  blocking collectives  22.4 us (23%)
  between operations  14.2 us (15%)
  matrix products  10.1 us (11%)
  other arithmetic  5.7 us (6%)
  local copies, waits for them, and re-layouts  1.33 us (1%)
    psum x1, waiting for transfers between devices, body(): lax.psum((jnp.sum(weights, axis=-1), local_values), 'seq')  22.5 us
    reduce_scatter x1, waiting for transfers between devices, body(): lax.psum_scatter(lax.dot_general(w_out, flattened, (((0,), (1,)), ((), ()...  18.7 us
    pmax x1, blocking collectives, body(): cache_top = lax.pmax(local_top, 'seq')  13.9 us
    psum x1, blocking collectives, body(): lax.psum((jnp.sum(weights, axis=-1), local_values), 'seq')  8.52 us
    dot_general x1, matrix products, body(): lax.dot_general(w_out, flattened, (((0,), (1,)), ((), ())), preferred_ele...  5.2 us
    dot_general x1, matrix products, body(): jnp.einsum('srkgt,rktd->srkgd', weights.astype(jnp.bfloat16), cache_value...  2.68 us
  transfers between devices with their start and end apart: 2, of which 2 were waited for; matrix products, arithmetic and copies ran while one was open for 2% of the time, Pallas kernels for 0%

commit v1 on v0

v1 whole, which is shorter than its diff:
```python
import functools
import math

import jax
import jax.numpy as jnp
from jax import lax
from jax.experimental import pallas as pl
from jax.experimental.pallas import tpu as pltpu
from jax.sharding import PartitionSpec as P

ROPE_BASE = 500000.0
FLOOR_SCORE = -1e30
FLOOR_TOP = -1e29
MESH = pl.DeviceIdType.MESH


def kernel(
    seq_n, head_n, dims,
    lengths, positions, queries, new_keys, new_values, keys_hbm, values_hbm, w_hbm,
    layer_out, cache_mass, new_mass,
    keys, values, w, gathered, weights, turned, att, part, landed,
    key_sem, value_sem, w_sem, seq_send, seq_recv, head_send, head_recv,
):
    steps_n, requests, kv_here, group, head_dim, local_len = dims
    rows = steps_n * group
    half = head_dim // 2
    seq_me = lax.axis_index("seq")
    head_me = lax.axis_index("head")

    fetches = {}
    for k in range(kv_here):
        for r in range(requests):
            p = k * requests + r
            fetches["k", p] = pltpu.make_async_copy(keys_hbm.at[r, k], keys.at[p], key_sem.at[p])
            fetches["v", p] = pltpu.make_async_copy(values_hbm.at[r, k], values.at[p], value_sem.at[p])
            fetches["k", p].start()
            fetches["v", p].start()
    depth = group * head_dim
    for k in range(kv_here):
        span = pl.ds(k * depth, depth)
        fetches["w", k] = pltpu.make_async_copy(w_hbm.at[span], w.at[span], w_sem.at[k])
        fetches["w", k].start()

    barrier = pltpu.get_barrier_semaphore()
    for d in range(1, seq_n):
        pl.semaphore_signal(barrier, inc=1, device_id={"seq": lax.rem(seq_me + d, seq_n)}, device_id_type=MESH)
    for d in range(1, head_n):
        pl.semaphore_signal(barrier, inc=1, device_id={"head": lax.rem(head_me + d, head_n)}, device_id_type=MESH)

    tokens = steps_n * requests
    row_at = lax.broadcasted_iota(jnp.int32, (tokens, head_dim), 0)
    lane_at = lax.broadcasted_iota(jnp.int32, (tokens, head_dim), 1)
    turns = jnp.zeros((tokens, head_dim), jnp.float32)
    for s in range(steps_n):
        for r in range(requests):
            moment = (positions[r] + s).astype(jnp.float32)
            turns = jnp.where(row_at == s * requests + r, moment, turns)
    index = jnp.where(lane_at < half, lane_at, lane_at - half).astype(jnp.float32)
    angles = turns * jnp.exp(index * (-2.0 * math.log(ROPE_BASE) / head_dim))
    cosine = jnp.cos(angles)
    sine = jnp.sin(angles)
    sine = jnp.where(lane_at < half, -sine, sine)

    def turn(x, at):
        return x * cosine[at : at + 1] + pltpu.roll(x, half, 1) * sine[at : at + 1]

    recent = {}
    for r in range(requests):
        turned_q = [turn(queries[s, r].astype(jnp.float32), s * requests + r) for s in range(steps_n)]
        for k in range(kv_here):
            q = jnp.concatenate([t[k * group : (k + 1) * group] for t in turned_q], axis=0).astype(jnp.bfloat16)
            turned[k * requests + r] = q
    inv_root = 1.0 / math.sqrt(head_dim)

    pl.semaphore_wait(barrier, seq_n + head_n - 2)

    stat_row = requests * rows
    lane = lax.broadcasted_iota(jnp.int32, (rows, head_dim), 1)
    slots = lax.broadcasted_iota(jnp.int32, (rows, local_len), 1) + seq_me * local_len
    seq_copies = {}
    for k in range(kv_here):
        stats = jnp.zeros((rows, head_dim), jnp.float32)
        for r in range(requests):
            p = k * requests + r
            fetches["k", p].wait()
            scores = lax.dot_general(
                turned[p], keys[p], (((1,), (1,)), ((), ())), preferred_element_type=jnp.float32
            ) * inv_root
            scores = jnp.where(slots < lengths[r], scores, FLOOR_SCORE)
            top = jnp.maximum(jnp.max(scores, axis=1, keepdims=True), FLOOR_TOP)
            weight = jnp.exp(scores - top)
            weights[p] = weight
            stats = jnp.where(lane == 2 * r, top, stats)
            stats = jnp.where(lane == 2 * r + 1, jnp.sum(weight, axis=1, keepdims=True), stats)
            fetches["v", p].wait()
            gathered[seq_me, k, pl.ds(r * rows, rows), :] = jnp.dot(
                weight.astype(jnp.bfloat16), values[p], preferred_element_type=jnp.float32
            )
        gathered[seq_me, k, pl.ds(stat_row, rows), :] = stats
        for d in range(1, seq_n):
            copy = pltpu.make_async_remote_copy(
                src_ref=gathered.at[seq_me, k],
                dst_ref=gathered.at[seq_me, k],
                send_sem=seq_send.at[k, d - 1],
                recv_sem=seq_recv.at[k, d - 1],
                device_id={"seq": lax.rem(seq_me + d, seq_n)},
                device_id_type=MESH,
            )
            copy.start()
            seq_copies[k, d] = copy

    step_at = lax.broadcasted_iota(jnp.int32, (rows, 1), 0)
    for k in range(kv_here):
        for r in range(requests):
            p = k * requests + r
            q = turned[p].astype(jnp.float32)
            for i in range(steps_n):
                key = turn(new_keys[i, r].astype(jnp.float32), i * requests + r)
                key = key[k : k + 1].astype(jnp.bfloat16).astype(jnp.float32)
                score = jnp.sum(q * key, axis=1, keepdims=True) * inv_root
                recent[p, i] = jnp.where(step_at >= i * group, score, FLOOR_SCORE)

    width = part.shape[2]
    factors = {}
    head_copies = {}

    def send(d):
        copy = pltpu.make_async_remote_copy(
            src_ref=part.at[lax.rem(head_me + d, head_n)],
            dst_ref=landed.at[d - 1],
            send_sem=head_send.at[d - 1],
            recv_sem=head_recv.at[d - 1],
            device_id={"head": lax.rem(head_me + d, head_n)},
            device_id_type=MESH,
        )
        copy.start()
        head_copies[d] = copy

    whole = None
    for k in range(kv_here):
        for d in range(1, seq_n):
            seq_copies[k, d].wait()
        stat = [gathered[j, k, pl.ds(stat_row, rows), :] for j in range(seq_n)]
        own_stat = gathered[seq_me, k, pl.ds(stat_row, rows), :]
        for r in range(requests):
            p = k * requests + r
            tops = [x[:, 2 * r : 2 * r + 1] for x in stat]
            highest = functools.reduce(jnp.maximum, tops + [recent[p, i] for i in range(steps_n)])
            total = jnp.zeros((rows, 1), jnp.float32)
            mixed = jnp.zeros((rows, head_dim), jnp.float32)
            for j in range(seq_n):
                scale = jnp.exp(tops[j] - highest)
                total += scale * stat[j][:, 2 * r + 1 : 2 * r + 2]
                mixed += scale * gathered[j, k, pl.ds(r * rows, rows), :]
            recents = []
            for i in range(steps_n):
                weight = jnp.exp(recent[p, i] - highest)
                recents.append(weight)
                total += weight
                value = new_values[i, r].astype(jnp.float32)[k : k + 1]
                mixed += weight.astype(jnp.bfloat16).astype(jnp.float32) * value
            attended = mixed / total
            share = lengths[r].astype(jnp.float32) / (steps_n * group)
            factors[p] = jnp.exp(own_stat[:, 2 * r : 2 * r + 1] - highest) / total * share
            for i in range(steps_n):
                new_mass[r, k : k + 1, i : i + 1] = jnp.sum(recents[i] / total, axis=0, keepdims=True) * share
            for s in range(steps_n):
                for g in range(group):
                    att[k * group + g, pl.ds(s * requests + r, 1), :] = attended[s * group + g : s * group + g + 1]
        block = jnp.concatenate([att[k * group + g] for g in range(group)], axis=1).astype(jnp.bfloat16)
        fetches["w", k].wait()
        last = k == kv_here - 1
        if width % 128 == 0:
            for d in list(range(1, head_n)) + [0]:
                chunk = lax.rem(head_me + d, head_n)
                product = jnp.dot(
                    block,
                    w[pl.ds(k * depth, depth), pl.ds(pl.multiple_of(chunk * width, width), width)],
                    preferred_element_type=jnp.float32,
                )
                part[chunk] = product if k == 0 else part[chunk] + product
                if last and d:
                    send(d)
        else:
            product = jnp.dot(block, w[pl.ds(k * depth, depth), :], preferred_element_type=jnp.float32)
            whole = product if k == 0 else whole + product
            if last:
                for c in range(head_n):
                    part[c] = whole[:, c * width : (c + 1) * width]
                for d in range(1, head_n):
                    send(d)

    for k in range(kv_here):
        for r in range(requests):
            p = k * requests + r
            cache_mass[r, k : k + 1, :] = jnp.sum(weights[p] * factors[p], axis=0, keepdims=True)

    summed = part[head_me]
    for d in range(1, head_n):
        head_copies[d].wait()
        summed += landed[d - 1]
    for s in range(steps_n):
        layer_out[s] = summed[s * requests : (s + 1) * requests].astype(jnp.bfloat16)


def body(seq_n, head_n, queries, cache_keys, cache_values, new_keys, new_values, w_out, lengths, positions):
    steps_n, requests, heads_here, head_dim = queries.shape
    kv_here, local_len = cache_keys.shape[1:3]
    group = heads_here // kv_here
    rows = steps_n * group
    pairs = kv_here * requests
    tokens = steps_n * requests
    width = w_out.shape[1] // head_n
    vmem = pl.BlockSpec(memory_space=pltpu.VMEM)
    smem = pl.BlockSpec(memory_space=pltpu.SMEM)
    hbm = pl.BlockSpec(memory_space=pl.ANY)
    f32, bf16 = jnp.float32, jnp.bfloat16
    dma = pltpu.SemaphoreType.DMA
    return pl.pallas_call(
        functools.partial(kernel, seq_n, head_n, (steps_n, requests, kv_here, group, head_dim, local_len)),
        out_shape=(
            jax.ShapeDtypeStruct((steps_n, requests, width), bf16),
            jax.ShapeDtypeStruct((requests, kv_here, local_len), f32),
            jax.ShapeDtypeStruct((requests, kv_here, steps_n), f32),
        ),
        in_specs=[smem, smem, vmem, vmem, vmem, hbm, hbm, hbm],
        out_specs=(vmem, vmem, vmem),
        scratch_shapes=[
            pltpu.VMEM((pairs, local_len, head_dim), bf16),
            pltpu.VMEM((pairs, local_len, head_dim), bf16),
            pltpu.VMEM(w_out.shape, bf16),
            pltpu.VMEM((seq_n, kv_here, (requests + 1) * rows, head_dim), f32),
            pltpu.VMEM((pairs, rows, local_len), f32),
            pltpu.VMEM((pairs, rows, head_dim), bf16),
            pltpu.VMEM((heads_here, tokens, head_dim), f32),
            pltpu.VMEM((head_n, tokens, width), f32),
            pltpu.VMEM((head_n - 1, tokens, width), f32),
            dma((pairs,)),
            dma((pairs,)),
            dma((kv_here,)),
            dma((kv_here, seq_n - 1)),
            dma((kv_here, seq_n - 1)),
            dma((head_n - 1,)),
            dma((head_n - 1,)),
        ],
        compiler_params=pltpu.CompilerParams(collective_id=0, has_side_effects=True),
    )(lengths, positions, queries, new_keys, new_values, cache_keys, cache_values, w_out)


def solution(mesh):
    return jax.shard_map(
        functools.partial(body, mesh.shape["seq"], mesh.shape["head"]),
        mesh=mesh,
        in_specs=(
            P(None, "rep", "head", None),
            P("rep", "head", "seq", None),
            P("rep", "head", "seq", None),
            P(None, "rep", "head", None),
            P(None, "rep", "head", None),
            P("head", "seq"),
            P("rep"),
            P("rep"),
        ),
        out_specs=(
            P(None, "rep", ("seq", "head")),
            P("rep", "head", "seq"),
            P("rep", "head", None),
        ),
        check_vma=False,
    )
```

time: 95.4 us -> 25.4 us (0.27)
  waiting for transfers between devices: 41.2 us -> 0 us
  blocking collectives: 22.4 us -> 0 us
  Pallas kernels: 0 us -> 20.4 us
  between operations: 14.2 us -> 0.64 us
  matrix products: 10.1 us -> 0 us
  other arithmetic: 5.7 us -> 0 us
  local copies, waits for them, and re-layouts: 1.33 us -> 4.01 us
    psum x1 -> x0, waiting for transfers between devices: 22.5 us -> none  [body(): lax.psum((jnp.sum(weights, axis=-1), local_values), 'seq')]
    pallas_call x0 -> x1, Pallas kernels: none -> 20.4 us  [body(): pl.pallas_call(functools.partial(kernel, seq_n, head_n, (steps_n, request...]
    reduce_scatter x1 -> x0, waiting for transfers between devices: 18.7 us -> none  [body(): lax.psum_scatter(lax.dot_general(w_out, flattened, (((0,), (1,)), ((), ()...]
    pmax x1 -> x0, blocking collectives: 13.9 us -> none  [body(): cache_top = lax.pmax(local_top, 'seq')]
    dot_general x5 -> x0, matrix products: 10.1 us -> none  [the longest x1 5.2 us: body(): lax.dot_general(w_out, flattened, (((0,), (1,)), ((), ())), preferred_ele...]
    psum x1 -> x0, blocking collectives: 8.52 us -> none  [body(): lax.psum((jnp.sum(weights, axis=-1), local_values), 'seq')]
    convert_element_type x4 -> x0, other arithmetic: 3.04 us -> none  [the longest x1 0.86 us: body(): moments = (positions[None, :] + offsets[:, None]).astype(jnp.float32)]
    unnamed x7 -> x2, local copies, waits for them, and re-layouts: 0.69 us -> 2.67 us
  transfers between devices with their start and end apart: 2 -> 0, of which waited for: 2 -> 0; matrix products, arithmetic and copies ran while one was open for 2% -> 0% of each run, Pallas kernels for 0% -> 0%
where the time goes in v1:
time: 25.4 us; the launch traced here: 25.1 us
  Pallas kernels  20.4 us (80%)
  local copies, waits for them, and re-layouts  4.01 us (16%)
  between operations  0.64 us (3%)
    pallas_call x1, Pallas kernels, body(): pl.pallas_call(functools.partial(kernel, seq_n, head_n, (steps_n, request...  20.4 us
    unnamed x2, local copies, waits for them, and re-layouts  2.67 us
    pallas_call x1, local copies, waits for them, and re-layouts, body(): pl.pallas_call(functools.partial(kernel, seq_n, head_n, (steps_n, request...  1.34 us

profile of v1, /device:TPU:0, one launch (start us, length us, event | category | flops | bytes accessed | tf_op | source)
XLA Modules:
  0.0 25.1 jit_solution(16958220233868269810)
XLA Ops:
  0.6 20.4 %shard_map.103 = (bf16[2,4,512]{2,1,0:T(4,128)(2,1)}, f32[4,2,1024]{2,1,0:T(2,128)}, f32[4,2,2]{2,1,0:T(2,128)}) custom-call(s32[4]{0:T(128)} %lengths.1, s32[4]{0:T(128)} %positions.1, bf16[2,4,16,128]{3,2,1,0:T(8,128)(2,1)} %queries.1, bf16[2,4,2,128]{3,2,1,0:T(2,128)(2,1)} %new_keys.1, bf16[2,4,2,128]{3,2,1,0:T(2,128)(2,1)} %new_values.1, ...), custom_call_target="tpu_custom_call" | custom-call | tf_op jit(solution)/shard_map/pallas_call | solution.py:219
  21.0 1.3 %copy.11 = f32[4,2,2]{0,2,1:T(2,128)} copy(f32[4,2,2]{2,1,0:T(2,128)} %get-tuple-element.5) | data formatting | bytes 128 | tf_op jit(solution)/shard_map/pallas_call | solution.py:219
  22.4 1.3 %copy.14 = bf16[2,4,512]{2,1,0:T(4,128)(2,1)} copy(bf16[2,4,512]{2,1,0:T(4,128)(2,1)} %get-tuple-element.9) | data formatting | bytes 16384
  23.7 1.4 %copy.15 = f32[4,2,1024]{2,1,0:T(2,128)} copy(f32[4,2,1024]{2,1,0:T(2,128)} %get-tuple-element.10) | data formatting | bytes 65536

commit v2 on v1

--- a/solution.py
+++ b/solution.py
@@ -11,15 +11,18 @@
 ROPE_BASE = 500000.0
 FLOOR_SCORE = -1e30
 FLOOR_TOP = -1e29
+BARRIER_AT = 0
+VMEM_GRANT = 66_000_000
+FINISH_GRANT = 66_000_000
 MESH = pl.DeviceIdType.MESH
 
 
 def kernel(
     seq_n, head_n, dims,
-    lengths, positions, queries, new_keys, new_values, keys_hbm, values_hbm, w_hbm,
-    layer_out, cache_mass, new_mass,
-    keys, values, w, gathered, weights, turned, att, part, landed,
-    key_sem, value_sem, w_sem, seq_send, seq_recv, head_send, head_recv,
+    lengths_hbm, positions_hbm, queries_hbm, new_keys_hbm, new_values_hbm, keys_hbm, values_hbm, w_hbm,
+    layer_sum, cache_mass, new_mass,
+    lengths, positions, queries, new_keys, new_values, keys, values, w, gathered, weights, turned, att, part, landed,
+    small_sem, key_sem, value_sem, w_sem, seq_send, seq_recv, head_send, head_recv,
 ):
     steps_n, requests, kv_here, group, head_dim, local_len = dims
     rows = steps_n * group
@@ -27,6 +30,20 @@
     seq_me = lax.axis_index("seq")
     head_me = lax.axis_index("head")
 
+    smalls = [
+        pltpu.make_async_copy(source, target, small_sem.at[n])
+        for n, (source, target) in enumerate(zip(
+            (positions_hbm, lengths_hbm, queries_hbm, new_keys_hbm, new_values_hbm),
+            (positions, lengths, queries, new_keys, new_values),
+        ))
+    ]
+    for copy in smalls:
+        copy.start()
+    barrier = pltpu.get_barrier_semaphore()
+    for d in range(1, seq_n):
+        pl.semaphore_signal(barrier, inc=1, device_id={"seq": lax.rem(seq_me + d, seq_n)}, device_id_type=MESH)
+    for d in range(1, head_n):
+        pl.semaphore_signal(barrier, inc=1, device_id={"head": lax.rem(head_me + d, head_n)}, device_id_type=MESH)
     fetches = {}
     for k in range(kv_here):
         for r in range(requests):
@@ -41,11 +58,8 @@
         fetches["w", k] = pltpu.make_async_copy(w_hbm.at[span], w.at[span], w_sem.at[k])
         fetches["w", k].start()
 
-    barrier = pltpu.get_barrier_semaphore()
-    for d in range(1, seq_n):
-        pl.semaphore_signal(barrier, inc=1, device_id={"seq": lax.rem(seq_me + d, seq_n)}, device_id_type=MESH)
-    for d in range(1, head_n):
-        pl.semaphore_signal(barrier, inc=1, device_id={"head": lax.rem(head_me + d, head_n)}, device_id_type=MESH)
+    for copy in smalls:
+        copy.wait()
 
     tokens = steps_n * requests
     row_at = lax.broadcasted_iota(jnp.int32, (tokens, head_dim), 0)
@@ -72,14 +86,28 @@
             turned[k * requests + r] = q
     inv_root = 1.0 / math.sqrt(head_dim)
 
-    pl.semaphore_wait(barrier, seq_n + head_n - 2)
-
     stat_row = requests * rows
-    lane = lax.broadcasted_iota(jnp.int32, (rows, head_dim), 1)
+    lane = lax.broadcasted_iota(jnp.int32, (group, head_dim), 1)
     slots = lax.broadcasted_iota(jnp.int32, (rows, local_len), 1) + seq_me * local_len
     seq_copies = {}
-    for k in range(kv_here):
-        stats = jnp.zeros((rows, head_dim), jnp.float32)
+
+    def share_piece(k, r):
+        p = k * requests + r
+        piece = gathered.at[seq_me, k, pl.ds(r * rows, rows if r < requests - 1 else rows + group)]
+        for d in range(1, seq_n):
+            copy = pltpu.make_async_remote_copy(
+                src_ref=piece,
+                dst_ref=piece,
+                send_sem=seq_send.at[p, d - 1],
+                recv_sem=seq_recv.at[p, d - 1],
+                device_id={"seq": lax.rem(seq_me + d, seq_n)},
+                device_id_type=MESH,
+            )
+            copy.start()
+            seq_copies[p, d] = copy
+
+    for k in range(kv_here):
+        stats = jnp.zeros((group, head_dim), jnp.float32)
         for r in range(requests):
             p = k * requests + r
             fetches["k", p].wait()
@@ -90,24 +118,24 @@
             top = jnp.maximum(jnp.max(scores, axis=1, keepdims=True), FLOOR_TOP)
             weight = jnp.exp(scores - top)
             weights[p] = weight
-            stats = jnp.where(lane == 2 * r, top, stats)
-            stats = jnp.where(lane == 2 * r + 1, jnp.sum(weight, axis=1, keepdims=True), stats)
+            total = jnp.sum(weight, axis=1, keepdims=True)
+            for s in range(steps_n):
+                column = 2 * (s * requests + r)
+                own = slice(s * group, (s + 1) * group)
+                stats = jnp.where(lane == column, top[own], stats)
+                stats = jnp.where(lane == column + 1, total[own], stats)
             fetches["v", p].wait()
             gathered[seq_me, k, pl.ds(r * rows, rows), :] = jnp.dot(
                 weight.astype(jnp.bfloat16), values[p], preferred_element_type=jnp.float32
             )
-        gathered[seq_me, k, pl.ds(stat_row, rows), :] = stats
-        for d in range(1, seq_n):
-            copy = pltpu.make_async_remote_copy(
-                src_ref=gathered.at[seq_me, k],
-                dst_ref=gathered.at[seq_me, k],
-                send_sem=seq_send.at[k, d - 1],
-                recv_sem=seq_recv.at[k, d - 1],
-                device_id={"seq": lax.rem(seq_me + d, seq_n)},
-                device_id_type=MESH,
-            )
-            copy.start()
-            seq_copies[k, d] = copy
+            if r == requests - 1:
+                gathered[seq_me, k, pl.ds(stat_row, group), :] = stats
+            if p == BARRIER_AT:
+                pl.semaphore_wait(barrier, seq_n + head_n - 2)
+                for earlier in range(p + 1):
+                    share_piece(*divmod(earlier, requests))
+            if p > BARRIER_AT:
+                share_piece(k, r)
 
     step_at = lax.broadcasted_iota(jnp.int32, (rows, 1), 0)
     for k in range(kv_here):
@@ -136,21 +164,26 @@
         copy.start()
         head_copies[d] = copy
 
+    def column_of(stat, r, which):
+        at = [2 * (s * requests + r) + which for s in range(steps_n)]
+        return jnp.concatenate([stat[:, c : c + 1] for c in at], axis=0)
+
     whole = None
     for k in range(kv_here):
-        for d in range(1, seq_n):
-            seq_copies[k, d].wait()
-        stat = [gathered[j, k, pl.ds(stat_row, rows), :] for j in range(seq_n)]
-        own_stat = gathered[seq_me, k, pl.ds(stat_row, rows), :]
-        for r in range(requests):
-            p = k * requests + r
-            tops = [x[:, 2 * r : 2 * r + 1] for x in stat]
+        for r in range(requests):
+            for d in range(1, seq_n):
+                seq_copies[k * requests + r, d].wait()
+        stat = [gathered[j, k, pl.ds(stat_row, group), :] for j in range(seq_n)]
+        own_stat = gathered[seq_me, k, pl.ds(stat_row, group), :]
+        for r in range(requests):
+            p = k * requests + r
+            tops = [column_of(x, r, 0) for x in stat]
             highest = functools.reduce(jnp.maximum, tops + [recent[p, i] for i in range(steps_n)])
             total = jnp.zeros((rows, 1), jnp.float32)
             mixed = jnp.zeros((rows, head_dim), jnp.float32)
             for j in range(seq_n):
                 scale = jnp.exp(tops[j] - highest)
-                total += scale * stat[j][:, 2 * r + 1 : 2 * r + 2]
+                total += scale * column_of(stat[j], r, 1)
                 mixed += scale * gathered[j, k, pl.ds(r * rows, rows), :]
             recents = []
             for i in range(steps_n):
@@ -161,9 +194,9 @@
                 mixed += weight.astype(jnp.bfloat16).astype(jnp.float32) * value
             attended = mixed / total
             share = lengths[r].astype(jnp.float32) / (steps_n * group)
-            factors[p] = jnp.exp(own_stat[:, 2 * r : 2 * r + 1] - highest) / total * share
+            factors[p] = jnp.exp(column_of(own_stat, r, 0) - highest) / total * share
             for i in range(steps_n):
-                new_mass[r, k : k + 1, i : i + 1] = jnp.sum(recents[i] / total, axis=0, keepdims=True) * share
+                new_mass[k, i : i + 1, r : r + 1] = jnp.sum(recents[i] / total, axis=0, keepdims=True) * share
             for s in range(steps_n):
                 for g in range(group):
                     att[k * group + g, pl.ds(s * requests + r, 1), :] = attended[s * group + g : s * group + g + 1]
@@ -199,8 +232,15 @@
     for d in range(1, head_n):
         head_copies[d].wait()
         summed += landed[d - 1]
+    layer_sum[...] = summed
+
+
+def finish(layer_sum, mass_in, new_in, layer_out, cache_mass, new_mass):
+    steps_n, requests = layer_out.shape[:2]
     for s in range(steps_n):
-        layer_out[s] = summed[s * requests : (s + 1) * requests].astype(jnp.bfloat16)
+        layer_out[s] = layer_sum[s * requests : (s + 1) * requests].astype(jnp.bfloat16)
+    cache_mass[...] = mass_in[...]
+    new_mass[...] = new_in[...]
 
 
 def body(seq_n, head_n, queries, cache_keys, cache_values, new_keys, new_values, w_out, lengths, positions):
@@ -212,39 +252,58 @@
     tokens = steps_n * requests
     width = w_out.shape[1] // head_n
     vmem = pl.BlockSpec(memory_space=pltpu.VMEM)
-    smem = pl.BlockSpec(memory_space=pltpu.SMEM)
-    hbm = pl.BlockSpec(memory_space=pl.ANY)
+    hbm = pl.BlockSpec(memory_space=pltpu.HBM)
     f32, bf16 = jnp.float32, jnp.bfloat16
     dma = pltpu.SemaphoreType.DMA
-    return pl.pallas_call(
+    summed, cache_mass, new_mass = pl.pallas_call(
         functools.partial(kernel, seq_n, head_n, (steps_n, requests, kv_here, group, head_dim, local_len)),
         out_shape=(
-            jax.ShapeDtypeStruct((steps_n, requests, width), bf16),
+            jax.ShapeDtypeStruct((tokens, width), f32),
             jax.ShapeDtypeStruct((requests, kv_here, local_len), f32),
-            jax.ShapeDtypeStruct((requests, kv_here, steps_n), f32),
-        ),
-        in_specs=[smem, smem, vmem, vmem, vmem, hbm, hbm, hbm],
+            jax.ShapeDtypeStruct((kv_here, steps_n, requests), f32),
+        ),
+        in_specs=[hbm] * 8,
         out_specs=(vmem, vmem, vmem),
         scratch_shapes=[
+            pltpu.SMEM(lengths.shape, jnp.int32),
+            pltpu.SMEM(positions.shape, jnp.int32),
+            pltpu.VMEM(queries.shape, bf16),
+            pltpu.VMEM(new_keys.shape, bf16),
+            pltpu.VMEM(new_values.shape, bf16),
             pltpu.VMEM((pairs, local_len, head_dim), bf16),
             pltpu.VMEM((pairs, local_len, head_dim), bf16),
             pltpu.VMEM(w_out.shape, bf16),
-            pltpu.VMEM((seq_n, kv_here, (requests + 1) * rows, head_dim), f32),
+            pltpu.VMEM((seq_n, kv_here, requests * rows + group, head_dim), f32),
             pltpu.VMEM((pairs, rows, local_len), f32),
             pltpu.VMEM((pairs, rows, head_dim), bf16),
             pltpu.VMEM((heads_here, tokens, head_dim), f32),
             pltpu.VMEM((head_n, tokens, width), f32),
             pltpu.VMEM((head_n - 1, tokens, width), f32),
+            dma((5,)),
             dma((pairs,)),
             dma((pairs,)),
             dma((kv_here,)),
-            dma((kv_here, seq_n - 1)),
-            dma((kv_here, seq_n - 1)),
+            dma((pairs, seq_n - 1)),
+            dma((pairs, seq_n - 1)),
             dma((head_n - 1,)),
             dma((head_n - 1,)),
         ],
-        compiler_params=pltpu.CompilerParams(collective_id=0, has_side_effects=True),
+        compiler_params=pltpu.CompilerParams(
+            collective_id=0, has_side_effects=True, vmem_limit_bytes=VMEM_GRANT
+        ),
     )(lengths, positions, queries, new_keys, new_values, cache_keys, cache_values, w_out)
+    layer_out, cache_mass, new_mass = pl.pallas_call(
+        finish,
+        out_shape=(
+            jax.ShapeDtypeStruct((steps_n, requests, width), bf16),
+            jax.ShapeDtypeStruct(cache_mass.shape, f32),
+            jax.ShapeDtypeStruct(new_mass.shape, f32),
+        ),
+        in_specs=[vmem] * 3,
+        out_specs=(vmem, vmem, vmem),
+        compiler_params=pltpu.CompilerParams(vmem_limit_bytes=FINISH_GRANT),
+    )(summed, cache_mass, new_mass)
+    return layer_out, cache_mass, jnp.transpose(new_mass, (2, 0, 1))
 
 
 def solution(mesh):

time: 25.4 us -> 20.6 us (0.81)
  local copies, waits for them, and re-layouts: 4.01 us -> 0 us
  Pallas kernels: 20.4 us -> 19.7 us
    unnamed x2 -> x0, local copies, waits for them, and re-layouts: 2.67 us -> none
    pallas_call x1, Pallas kernels: 20.4 us -> 18.3 us  [body(): pl.pallas_call(functools.partial(kernel, seq_n, head_n, (steps_n, request...]
    pallas_call x0 -> x1, Pallas kernels: none -> 1.38 us  [body(): pl.pallas_call(finish, out_shape=(jax.ShapeDtypeStruct((steps_n, requests...]
    pallas_call x1 -> x0, local copies, waits for them, and re-layouts: 1.34 us -> none  [body(): pl.pallas_call(functools.partial(kernel, seq_n, head_n, (steps_n, request...]
where the time goes in v2:
time: 20.6 us; the launch traced here: 20.4 us
  Pallas kernels  19.7 us (96%)
  between operations  0.64 us (3%)
    pallas_call x1, Pallas kernels, body(): pl.pallas_call(functools.partial(kernel, seq_n, head_n, (steps_n, request...  18.3 us
    pallas_call x1, Pallas kernels, body(): pl.pallas_call(finish, out_shape=(jax.ShapeDtypeStruct((steps_n, requests...  1.38 us

profile of v2, /device:TPU:0, one launch (start us, length us, event | category | flops | bytes accessed | tf_op | source)
XLA Modules:
  0.0 20.4 jit_solution(11321442808080284071)
XLA Ops:
  0.6 18.3 %shard_map.103 = (f32[8,512]{1,0:T(8,128)}, f32[4,2,1024]{2,1,0:T(2,128)}, f32[2,2,4]{2,1,0:T(2,128)}) custom-call(s32[4]{0:T(128)} %lengths_hbm.1, s32[4]{0:T(128)} %positions_hbm.1, bf16[2,4,16,128]{3,2,1,0:T(8,128)(2,1)} %queries_hbm.1, bf16[2,4,2,128]{3,2,1,0:T(2,128)(2,1)} %new_keys_hbm.1, bf16[2,4,2,128]{3,2,1,0:T(2,128)(2,1)} %new_values_hbm.1, ...), custom_call_target="tpu_custom_call" | custom-call | tf_op jit(solution)/shard_map/pallas_call | solution.py:258
  19.0 1.4 %shard_map.104 = (bf16[2,4,512]{2,1,0:T(4,128)(2,1)}, f32[4,2,1024]{2,1,0:T(2,128)}, f32[2,2,4]{2,1,0:T(2,128)}) custom-call(f32[8,512]{1,0:T(8,128)} %get-tuple-element.9.layer_sum, f32[4,2,1024]{2,1,0:T(2,128)} %get-tuple-element.10.mass_in, f32[2,2,4]{2,1,0:T(2,128)} %get-tuple-element.11.new_in), custom_call_target="tpu_custom_call" | custom-call | tf_op jit(solution)/shard_map/pallas_call | solution.py:295

commit v3 on v2

--- a/solution.py
+++ b/solution.py
@@ -12,9 +12,14 @@
 FLOOR_SCORE = -1e30
 FLOOR_TOP = -1e29
 BARRIER_AT = 0
-VMEM_GRANT = 66_000_000
-FINISH_GRANT = 66_000_000
+FETCH_AT = 0
+VMEM_GRANT = 64_000_000
+FINISH_GRANT = 8_000_000
 MESH = pl.DeviceIdType.MESH
+
+
+def far_first(n):
+    return sorted(range(1, n), key=lambda d: -min(d, n - d))
 
 
 def kernel(
@@ -56,7 +61,6 @@
     for k in range(kv_here):
         span = pl.ds(k * depth, depth)
         fetches["w", k] = pltpu.make_async_copy(w_hbm.at[span], w.at[span], w_sem.at[k])
-        fetches["w", k].start()
 
     for copy in smalls:
         copy.wait()
@@ -94,7 +98,7 @@
     def share_piece(k, r):
         p = k * requests + r
         piece = gathered.at[seq_me, k, pl.ds(r * rows, rows if r < requests - 1 else rows + group)]
-        for d in range(1, seq_n):
+        for d in far_first(seq_n):
             copy = pltpu.make_async_remote_copy(
                 src_ref=piece,
                 dst_ref=piece,
@@ -111,6 +115,9 @@
         for r in range(requests):
             p = k * requests + r
             fetches["k", p].wait()
+            if p == FETCH_AT:
+                for n in range(kv_here):
+                    fetches["w", n].start()
             scores = lax.dot_general(
                 turned[p], keys[p], (((1,), (1,)), ((), ())), preferred_element_type=jnp.float32
             ) * inv_root
@@ -258,9 +265,9 @@
     summed, cache_mass, new_mass = pl.pallas_call(
         functools.partial(kernel, seq_n, head_n, (steps_n, requests, kv_here, group, head_dim, local_len)),
         out_shape=(
-            jax.ShapeDtypeStruct((tokens, width), f32),
-            jax.ShapeDtypeStruct((requests, kv_here, local_len), f32),
-            jax.ShapeDtypeStruct((kv_here, steps_n, requests), f32),
+            pltpu.VMEM((tokens, width), f32),
+            pltpu.VMEM((requests, kv_here, local_len), f32),
+            pltpu.VMEM((kv_here, steps_n, requests), f32),
         ),
         in_specs=[hbm] * 8,
         out_specs=(vmem, vmem, vmem),

time: 20.6 us -> 19.2 us (0.932)
  Pallas kernels: 19.7 us -> 18.3 us
    pallas_call x1, Pallas kernels: 1.38 us -> 0.62 us  [body(): pl.pallas_call(finish, out_shape=(jax.ShapeDtypeStruct((steps_n, requests...]
    pallas_call x1, Pallas kernels: 18.3 us -> 17.7 us  [body(): pl.pallas_call(functools.partial(kernel, seq_n, head_n, (steps_n, request...]
where the time goes in v3:
time: 19.2 us; the launch traced here: 19 us
  Pallas kernels  18.3 us (95%)
  between operations  0.64 us (3%)
    pallas_call x1, Pallas kernels, body(): pl.pallas_call(functools.partial(kernel, seq_n, head_n, (steps_n, request...  17.7 us
    pallas_call x1, Pallas kernels, body(): pl.pallas_call(finish, out_shape=(jax.ShapeDtypeStruct((steps_n, requests...  0.62 us

profile of v3, /device:TPU:0, one launch (start us, length us, event | category | flops | bytes accessed | tf_op | source)
XLA Modules:
  0.0 19.0 jit_solution(3734864273987886029)
XLA Ops:
  0.6 17.7 %shard_map.103 = (f32[8,512]{1,0:T(8,128)S(1)}, f32[4,2,1024]{2,1,0:T(2,128)S(1)}, f32[2,2,4]{2,1,0:T(2,128)S(1)}) custom-call(s32[4]{0:T(128)} %lengths_hbm.1, s32[4]{0:T(128)} %positions_hbm.1, bf16[2,4,16,128]{3,2,1,0:T(8,128)(2,1)} %queries_hbm.1, bf16[2,4,2,128]{3,2,1,0:T(2,128)(2,1)} %new_keys_hbm.1, bf16[2,4,2,128]{3,2,1,0:T(2,128)(2,1)} %new_values_hbm.1, ...), custom_call_target="tpu_custom_call" | custom-call | tf_op jit(solution)/shard_map/pallas_call | solution.py:265
  18.4 0.6 %shard_map.104 = (bf16[2,4,512]{2,1,0:T(4,128)(2,1)}, f32[4,2,1024]{2,1,0:T(2,128)}, f32[2,2,4]{2,1,0:T(2,128)}) custom-call(f32[8,512]{1,0:T(8,128)S(1)} %get-tuple-element.9.layer_sum, f32[4,2,1024]{2,1,0:T(2,128)S(1)} %get-tuple-element.10.mass_in, f32[2,2,4]{2,1,0:T(2,128)S(1)} %get-tuple-element.11.new_in), custom_call_target="tpu_custom_call" | custom-call | tf_op jit(solution)/shard_map/pallas_call | solution.py:302
